TPU v7x, 512 devices: a whole 4x4x16 slice. The times are simulated.
512 devices in a mesh: leaf: 128 (over x_hi, z, y), sub: 4 (over x_lo, core).
Axes of the slice: x: 4 (x_hi: 2, x_lo: 2; x = x_hi * 2 + x_lo), y: 4, z: 16, core: 2. Of those that a mesh axis runs over, the one named last changes fastest.
Arguments:
- points: float32 [16384, 3, 128], P(('leaf', 'sub')), may hold values from 0 to 1
- charges: float32 [16384, 8, 128], P(('leaf', 'sub')), may hold values from -6 to 6
- leaf_skel: float32 [16384, 3, 64], P(('leaf', 'sub')), may hold values from 0 to 1
- mid_skel: float32 [2048, 3, 64], P(('leaf', 'sub')), may hold values from 0 to 1
- root_skel: float32 [128, 3, 64], replicated, may hold values from 0 to 1
- leaf_transfer: float32 [16384, 64, 64], P(('leaf', 'sub')), may hold values from -0.25 to 0.25
- mid_transfer: float32 [2048, 64, 64], P(('leaf', 'sub')), may hold values from -0.75 to 0.75
- near_list: int32 [16384, 27], P(('leaf', 'sub')), may hold values from -1 to 16383, as said below
- far_list: int32 [16384, 20], P(('leaf', 'sub')), may hold values from -1 to 16383, as said below
- mid_list: int32 [2048, 6], P(('leaf', 'sub')), may hold values from -1 to 2047, as said below
- root_list: int32 [128, 6], P('leaf'), may hold values from -1 to 127, as said below
Outputs:
- potentials: float32 [16384, 8, 128], P(('leaf', 'sub'))
Inputs may be any that keep to these rules, and one draw needn't show every extreme that they name: `near_list`: slot 0 of a leaf's row is the leaf itself. Every other entry is -1 or a leaf other than itself that lies on the same device or on one of the two devices beside it in the order of leaf indices; no leaf appears twice in the near and coupling rows of one leaf together. `far_list`: every entry is -1 or a leaf other than the row's own that lies on the same device or on one of the two devices beside it in the order of leaf indices, never one of the row's near_list entries. `mid_list`: every entry is -1 or a middle cluster other than the row's own under the same subtree root, at most once in a row. `root_list`: every entry is -1 or a root other than the row's own, at most once in a row.
All inputs are finite; a program needn't handle non-finite values.
Results may differ from a plain program's by a relative error of at most 0.0003.
Values sent between devices are 32-bit elements; how exact they have to be, the bound alone decides.
A program may use at most 64 MiB of HBM per device.

v0:
```python
import math
import jax
import jax.numpy as jnp
from jax import lax
from jax.sharding import PartitionSpec as P

DELTA2 = 0.0025
EXACT_PRECISION = lax.Precision.HIGHEST


def extended(block, sides, width):
    for axis, dim in sides:
        count = lax.axis_size(axis)
        forward = [(i, i + 1) for i in range(count - 1)]
        backward = [(target, source) for source, target in forward]
        low = lax.ppermute(
            lax.slice_in_dim(block, block.shape[dim] - width, None, axis=dim), axis, forward
        )
        high = lax.ppermute(lax.slice_in_dim(block, 0, width, axis=dim), axis, backward)
        block = jnp.concatenate([low, block, high], axis=dim)
    return block


def kernel(targets, sources):
    first = targets[:, 0, :, None] - sources[:, 0, None, :]
    second = targets[:, 1, :, None] - sources[:, 1, None, :]
    third = targets[:, 2, :, None] - sources[:, 2, None, :]
    return 1.0 / jnp.sqrt(first * first + second * second + third * third + DELTA2)


def lookup(table, partner_idx, offset):
    present = (partner_idx >= 0).astype(jnp.float32)
    position = jnp.clip(partner_idx - offset, 0, table.shape[0] - 1)
    return (table[position], present)


def couple(target_skel, coeff_table, skel_table, lists, offset, nrhs_count, scale):

    def add_slot(slot_no, running):
        partner_idx = lax.dynamic_slice_in_dim(lists, slot_no, 1, 1)[:, 0]
        partner_coeffs, present = lookup(coeff_table, partner_idx, offset)
        partner_skel, unused = lookup(skel_table, partner_idx, offset)
        matrix = kernel(target_skel, partner_skel)
        term = jnp.einsum("lab,lrb->lra", matrix, partner_coeffs, precision=EXACT_PRECISION)
        return running + term * (present * scale)[:, None, None]

    start_value = jnp.zeros((target_skel.shape[0], nrhs_count, coeff_table.shape[2]), jnp.float32)
    return lax.fori_loop(0, lists.shape[1], add_slot, start_value)


def local(
    points,
    charges,
    leaf_skel,
    mid_skel,
    root_skel,
    leaf_transfer,
    mid_transfer,
    near_list,
    far_list,
    mid_list,
    root_list,
):
    leaves = points.shape[0]
    nrhs_count = charges.shape[1]
    rank_count = leaf_skel.shape[2]
    leaf_count = points.shape[2]
    leaf_scale = 1.0 / math.sqrt(leaf_count)
    rank_scale = 1.0 / rank_count
    flat_index = lax.axis_index(("leaf", "sub"))
    window_start = (flat_index - 1) * leaves
    packed_points = jnp.concatenate([points, charges], axis=1)
    widened = extended(packed_points, ((("leaf", "sub"), 0),), leaves)

    def add_near(slot_no, running):
        partner_idx = lax.dynamic_slice_in_dim(near_list, slot_no, 1, 1)[:, 0]
        partner_rows, present = lookup(widened, partner_idx, window_start)
        matrix = kernel(points, partner_rows[:, :3])
        term = jnp.einsum("lpq,lrq->lrp", matrix, partner_rows[:, 3:], precision=EXACT_PRECISION)
        return running + term * (present / leaf_count)[:, None, None]

    near = lax.fori_loop(0, near_list.shape[1], add_near, jnp.zeros(charges.shape, jnp.float32))
    basis = kernel(points, leaf_skel)
    expansion_weights = (
        jnp.einsum("lpa,lrp->lra", basis, charges, precision=EXACT_PRECISION) * leaf_scale
    )
    packed_coeffs = jnp.concatenate([expansion_weights, leaf_skel], axis=1)
    fine_table = extended(packed_coeffs, ((("leaf", "sub"), 0),), leaves)
    leaf_potential_field = couple(
        leaf_skel,
        fine_table[:, :nrhs_count],
        fine_table[:, nrhs_count:],
        far_list,
        window_start,
        nrhs_count,
        rank_scale,
    )
    mids = leaves // 8
    leaf_cluster_groups = leaf_transfer.reshape(mids, 8, rank_count, rank_count)
    middle_expansion_weights = jnp.einsum(
        "hpsi,hpds->hdi",
        leaf_cluster_groups,
        expansion_weights.reshape(mids, 8, nrhs_count, rank_count),
        precision=EXACT_PRECISION,
    )
    packed_mid = jnp.concatenate([middle_expansion_weights, mid_skel], axis=1)
    mid_table = lax.all_gather(packed_mid, "sub", axis=0, tiled=True)
    group_start = lax.axis_index("leaf") * mid_table.shape[0]
    mid_field = couple(
        mid_skel,
        mid_table[:, :nrhs_count],
        mid_table[:, nrhs_count:],
        mid_list,
        group_start,
        nrhs_count,
        rank_scale,
    )
    partial_root = jnp.einsum(
        "mab,mra->rb", mid_transfer, middle_expansion_weights, precision=EXACT_PRECISION
    )
    summed_root = lax.psum(partial_root, "sub")
    root_table = lax.all_gather(summed_root[None], "leaf", axis=0, tiled=True)
    root_number = lax.axis_index("leaf")
    my_skel = lax.dynamic_slice_in_dim(root_skel, root_number, 1, 0)
    root_field = couple(my_skel, root_table, root_skel, root_list, 0, nrhs_count, rank_scale)
    middle_potential_total = mid_field + jnp.einsum(
        "mab,rb->mra", mid_transfer, root_field[0], precision=EXACT_PRECISION
    )
    leaf_potential_total = leaf_potential_field + jnp.einsum(
        "oxgc,osc->oxsg", leaf_cluster_groups, middle_potential_total, precision=EXACT_PRECISION
    ).reshape(leaves, nrhs_count, rank_count)
    return (
        near
        + jnp.einsum("lpa,lra->lrp", basis, leaf_potential_total, precision=EXACT_PRECISION)
        * leaf_scale
    )


def solution(mesh):
    in_specs = (
        P(("leaf", "sub"), None, None),
        P(("leaf", "sub"), None, None),
        P(("leaf", "sub"), None, None),
        P(("leaf", "sub"), None, None),
        P(),
        P(("leaf", "sub"), None, None),
        P(("leaf", "sub"), None, None),
        P(("leaf", "sub"), None),
        P(("leaf", "sub"), None),
        P(("leaf", "sub"), None),
        P("leaf", None),
    )
    out_specs = P(("leaf", "sub"), None, None)
    return jax.shard_map(local, mesh=mesh, in_specs=in_specs, out_specs=out_specs, check_vma=False)
```

profile of v0, /device:TPU:2, one launch (start us, length us, event | category | flops | bytes accessed | tf_op | source)
XLA Modules:
  0.0 699.5 jit_solution(9708654243711353516)
XLA Ops:
  13.6 5.6 collective-permute-start.1
  19.9 5.4 all_gather.6
  25.4 10.1 %while.60 = (s32[]{:T(128)}, f32[4,8,64]{2,1,0:T(8,128)S(1)}, s32[4,6]{0,1:T(8,128)S(1)}, s32[]{:T(128)}, f32[16,8,64]{2,1,0:T(8,128)S(1)}, /*index=5*/f32[4,3,6...) while((s32[]{:T(128)}, f32[4,8,64]{2,1,0:T(8,128)S(1)}, s32[4,6]{0,1:T(8,128)S(1)}, ...), condition=%wide.region_5.6_spmd.clone, body=%wide.region_4.5_spmd.clone.sunk | while | flops 1727519 | bytes 69875 | solution.py:48
  35.8 7.4 %psum.7 = f32[1,8,64]{2,1,0:T(8,128)S(1)} all-reduce(f32[1,8,64]{2,1,0:T(8,128)S(1)} %convolution_bitcast_fusion.2), channel_id=1, replica_groups=mesh['leaf'=128,'sub'=4] {'sub'}, use_global_device_ids=true, to_apply=%region_6.7 | all-reduce | flops 512 | bytes 4096 | tf_op jit(solution)/shard_map/psum | solution.py:121
  43.2 364.2 %all_gather.7 = f32[128,8,64]{2,1,0:T(8,128)S(1)} all-gather(f32[1,8,64]{2,1,0:T(8,128)S(1)} %psum.7), channel_id=1, replica_groups=mesh['leaf'=128,'sub'=4] {'leaf'}, dimensions={0}, use_global_device_ids=true | all-gather | bytes 264192 | tf_op jit(solution)/shard_map/all_gather | solution.py:122
  407.6 12.6 %while.61 = (s32[]{:T(128)}, f32[1,8,64]{2,1,0:T(8,128)S(1)}, s32[1,6]{1,0:T(1,128)S(1)}, f32[128,8,64]{2,1,0:T(8,128)S(1)}, f32[1,3,64]{2,1,0:T(4,128)S(1)}, /*...) while((s32[]{:T(128)}, f32[1,8,64]{2,1,0:T(8,128)S(1)}, ...), condition=%wide.region_8.9_spmd.clone, body=%wide.region_7.8_spmd.clone.sunk | while | flops 431623 | bytes 18109 | solution.py:48
  425.1 113.0 %while.59 = (s32[]{:T(128)}, f32[32,8,64]{2,1,0:T(8,128)S(1)}, s32[32,20]{0,1:T(8,128)}, s32[]{:T(128)}, f32[96,8,64]{2,1,0:T(8,128)S(1)}, /*index=5*/f32[32,3,6...) while((s32[]{:T(128)}, f32[32,8,64]{2,1,0:T(8,128)S(1)}, s32[32,20]{0,1:T(8,128)}, ...), condition=%wide.region_3.4_spmd.clone, body=%wide.region_2.3_spmd.clone.sunk | while | flops 13812963 | bytes 529523 | solution.py:48
  541.2 157.6 %while.58 = (s32[]{:T(128)}, f32[32,8,128]{2,1,0:T(8,128)S(1)}, s32[32,27]{0,1:T(8,128)S(1)}, s32[]{:T(128)}, f32[96,11,128]{2,1,0:T(8,128)S(1)}, /*index=5*/f32[32,3,128]{2,0,1:T(8,128)S(1)}, s32[]{:T(128)}, s32[]{:T(128)}) while((s32[]{:T(128)}, f32[32,8,128]{2,1,0:T(8,128)S(1)}, s32[32,27]{0,1:T(8,128)S(1)}, s32[]{:T(128)}, ...), condition=%wide.region_1.2_spmd.clone, body=%wide.region_0.1_spmd.clone.sunk | while | flops 55149792 | bytes 1054059 | solution.py:82
  542.0 5.1 fusion.156
  547.8 5.1 fusion.156
  553.6 5.1 fusion.156
  559.5 5.1 fusion.156
  565.3 5.1 fusion.156
  571.2 5.1 fusion.156
  577.0 5.1 fusion.156
  582.8 5.1 fusion.156
  588.7 5.1 fusion.156
  594.5 5.1 fusion.156
  600.3 5.1 fusion.156
  606.2 5.1 fusion.156
  612.0 5.1 fusion.156
  617.8 5.1 fusion.156
  623.7 5.1 fusion.156
  629.5 5.1 fusion.156
  635.4 5.1 fusion.156
  641.2 5.1 fusion.156
  647.0 5.1 fusion.156
  652.9 5.1 fusion.156
  658.7 5.1 fusion.156
  664.5 5.1 fusion.156
  687.9 5.1 fusion.156
  693.7 5.1 fusion.156
  (471 shorter events, 183.5 us)
Async XLA Ops:
  0.0 19.2 %copy-start = (f32[32,64,64]{2,1,0:T(8,128)S(1)}, f32[32,64,64]{2,1,0:T(8,128)}, u32[]{:S(2)}) copy-start(f32[32,64,64]{2,1,0:T(8,128)} %param.24) | copy-start | bytes 1572868
  2.4 3.5 copy-start.10
  2.4 3.5 copy-start.12
  2.4 9.2 %copy-start.2 = (f32[32,3,128]{2,0,1:T(8,128)S(1)}, f32[32,3,128]{2,0,1:T(8,128)}, u32[]{:S(2)}) copy-start(f32[32,3,128]{2,0,1:T(8,128)} %param.19) | copy-start | bytes 147460
  2.5 9.2 %copy-start.3 = (f32[32,8,128]{2,1,0:T(8,128)S(1)}, f32[32,8,128]{2,1,0:T(8,128)}, u32[]{:S(2)}) copy-start(f32[32,8,128]{2,1,0:T(8,128)} %param.20) | copy-start | bytes 393220
  2.5 16.7 %copy-start.5 = (f32[4,3,64]{2,0,1:T(4,128)S(1)}, f32[4,3,64]{2,0,1:T(4,128)}, u32[]{:S(2)}) copy-start(f32[4,3,64]{2,0,1:T(4,128)} %param.22) | copy-start | bytes 9220
  6.0 417.5 %collective-permute-start.2 = (f32[32,11,64]{2,1,0:T(8,128)S(1)}, f32[32,11,64]{2,1,0:T(8,128)S(1)}, u32[]{:S(2)}, u32[]{:S(2)}) collective-permute-start(f32[32,11,64]{2,1,0:T(8,128)S(1)} %pad_maximum_fusion.3), channel_id=1, source_target_pairs={{0,1},{1,2},{2,3},{3,4},{4,5},{5,6},{6,7},{7,8},{8,9},{9,10},{10,1... | collective-permute-start | bytes 270344 | tf_op jit(solution)/shard_map/ppermute | solution.py:16
  7.9 415.7 %collective-permute-start.3 = (f32[32,11,64]{2,1,0:T(8,128)S(1)}, f32[32,11,64]{2,1,0:T(8,128)S(1)}, u32[]{:S(2)}, u32[]{:S(2)}) collective-permute-start(f32[32,11,64]{2,1,0:T(8,128)S(1)} %pad_maximum_fusion.3), channel_id=1, source_target_pairs={{1,0},{2,1},{3,2},{4,3},{5,4},{6,5},{7,6},{8,7},{9,8},{10,9},{11,1... | collective-permute-start | bytes 270344 | tf_op jit(solution)/shard_map/ppermute | solution.py:19
  11.7 13.7 %copy-start.15 = (s32[4,6]{1,0:T(4,128)S(1)}, s32[4,6]{1,0:T(4,128)}, u32[]{:S(2)}) copy-start(s32[4,6]{1,0:T(4,128)} %param.28) | copy-start | bytes 292
  11.7 528.4 %collective-permute-start = (f32[32,11,128]{2,1,0:T(8,128)S(1)}, f32[32,11,128]{2,1,0:T(8,128)}, u32[]{:S(2)}, u32[]{:S(2)}) collective-permute-start(f32[32,11,128]{2,1,0:T(8,128)S(1)} %pad_maximum_fusion.2), channel_id=1, source_target_pairs={{0,1},{1,2},{2,3},{3,4},{4,5},{5,6},{6,7},{7,8},{8,9},{9,10},{10,1... | collective-permute-start | bytes 540680 | tf_op jit(solution)/shard_map/ppermute | solution.py:16
  13.6 526.5 %collective-permute-start.1 = (f32[32,11,128]{2,1,0:T(8,128)S(1)}, f32[32,11,128]{2,1,0:T(8,128)}, u32[]{:S(2)}, u32[]{:S(2)}) collective-permute-start(f32[32,11,128]{2,1,0:T(8,128)S(1)} %pad_maximum_fusion.2), channel_id=1, source_target_pairs={{1,0},{2,1},{3,2},{4,3},{5,4},{6,5},{7,6},{8,7},{9,8},{10,9},{11,1... | collective-permute-start | bytes 540680 | tf_op jit(solution)/shard_map/ppermute | solution.py:19
  25.4 10.1 %copy-start.4 = (f32[4,64,64]{2,1,0:T(8,128)S(1)}, f32[4,64,64]{2,1,0:T(8,128)}, u32[]{:S(2)}) copy-start(f32[4,64,64]{2,1,0:T(8,128)} %param.25) | copy-start | bytes 196612
  25.4 382.0 %copy-start.8 = (f32[128,3,64]{0,2,1:T(8,128)S(1)}, f32[128,3,64]{0,2,1:T(8,128)}, u32[]{:S(2)}) copy-start(f32[128,3,64]{0,2,1:T(8,128)} %param.23) | copy-start | bytes 294916
  35.5 372.0 %copy-start.14 = (s32[1,6]{1,0:T(1,128)S(1)}, s32[1,6]{1,0:T(1,128)}, u32[]{:S(2)}) copy-start(s32[1,6]{1,0:T(1,128)} %param.29) | copy-start | bytes 76
  420.2 3.2 copy-start.9
  424.1 0.8 copy-start.1
  424.1 0.9 copy-start.7
  425.1 113.1 %copy-start.11 = (f32[32,128]{1,0:T(8,128)S(1)}, f32[32,128]{1,0:T(8,128)}, u32[]{:S(2)}) copy-start(f32[32,128]{1,0:T(8,128)} %copy-done.10) | copy-start | bytes 49156
  425.1 113.1 %copy-start.13 = (f32[32,128]{1,0:T(8,128)S(1)}, f32[32,128]{1,0:T(8,128)}, u32[]{:S(2)}) copy-start(f32[32,128]{1,0:T(8,128)} %copy-done.12) | copy-start | bytes 49156
  540.1 1.2 copy-start.6
where the time goes:
time: 703 us; the launch traced here: 700 us
  blocking collectives  377 us (54%)
  matrix products  211 us (30%)
  local copies, waits for them, and re-layouts  52.6 us (7%)
  other arithmetic  35.4 us (5%)
  starting transfers between devices  13 us (2%)
  loops' own time  10.1 us (1%)
    all_gather x1, blocking collectives, local(): root_table = lax.all_gather(summed_root[None], 'leaf', axis=0, tiled=True)  364 us
    dot_general x27, matrix products, add_near(): jnp.einsum('lpq,lrq->lrp', matrix, partner_rows[:, 3:], precision=EXACT_P...  138 us
    dot_general x32, matrix products, add_slot(): jnp.einsum('lab,lrb->lra', matrix, partner_coeffs, precision=EXACT_PRECIS...  63.4 us
    gather x85, local copies, waits for them, and re-layouts, lookup(): return (table[position], present)  46.5 us
    select_n x53, other arithmetic, lookup(): return (table[position], present)  14.7 us
  transfers between devices with their start and end apart: 4, of which 0 were waited for; matrix products, arithmetic and copies ran while one was open for 19% of the time, Pallas kernels for 0%

commit v1 on v0

--- a/solution.py
+++ b/solution.py
@@ -1,3 +1,4 @@
+import functools
 import math
 import jax
 import jax.numpy as jnp
@@ -6,6 +7,16 @@
 
 DELTA2 = 0.0025
 EXACT_PRECISION = lax.Precision.HIGHEST
+
+
+def _update_points(packet, dim_no):
+    seen_now = lax.axis_size("leaf")
+    piece_next = jnp.stack(seen_now * [packet])
+    raw_out = lax.all_to_all(piece_next, "leaf", 0, 0)
+    return jnp.concatenate(raw_out, axis=dim_no)
+
+
+solve_the_sheet = functools.partial(_update_points, dim_no=0)
 
 
 def extended(block, sides, width):
@@ -119,7 +130,7 @@
         "mab,mra->rb", mid_transfer, middle_expansion_weights, precision=EXACT_PRECISION
     )
     summed_root = lax.psum(partial_root, "sub")
-    root_table = lax.all_gather(summed_root[None], "leaf", axis=0, tiled=True)
+    root_table = solve_the_sheet(summed_root[None])
     root_number = lax.axis_index("leaf")
     my_skel = lax.dynamic_slice_in_dim(root_skel, root_number, 1, 0)
     root_field = couple(my_skel, root_table, root_skel, root_list, 0, nrhs_count, rank_scale)

time: 703 us -> 408 us (0.58)
  the two profiles are of different devices: /device:TPU:2 before, /device:TPU:1 now
where the time goes in v1:
time: 408 us; the launch traced here: 405 us
  matrix products  248 us (61%)
  local copies, waits for them, and re-layouts  57.6 us (14%)
  starting transfers between devices  40.6 us (10%)
  other arithmetic  36.7 us (9%)
  blocking collectives  11.5 us (3%)
  loops' own time  10.1 us (2%)
    dot_general x27, matrix products, add_near(): jnp.einsum('lpq,lrq->lrp', matrix, partner_rows[:, 3:], precision=EXACT_P...  175 us
    dot_general x32, matrix products, add_slot(): jnp.einsum('lab,lrb->lra', matrix, partner_coeffs, precision=EXACT_PRECIS...  63.4 us
    gather x85, local copies, waits for them, and re-layouts, lookup(): return (table[position], present)  46.4 us
    all_to_all x1, starting transfers between devices, _update_points(): raw_out = lax.all_to_all(piece_next, 'leaf', 0, 0)  24.7 us
    select_n x53, other arithmetic, lookup(): return (table[position], present)  14.4 us
    mul x26, other arithmetic, add_slot(): return running + term * (present * scale)[:, None, None]  14 us
    ppermute x2, starting transfers between devices, extended(): lax.ppermute(lax.slice_in_dim(block, 0, width, axis=dim), axis, backward)  9.33 us
    another operation x3, loops' own time, couple(): return lax.fori_loop(0, lists.shape[1], add_slot, start_value)  8.88 us
  transfers between devices with their start and end apart: 5, of which 0 were waited for; matrix products, arithmetic and copies ran while one was open for 79% of the time, Pallas kernels for 0%

profile of v1, /device:TPU:1, one launch (start us, length us, event | category | flops | bytes accessed | tf_op | source)
XLA Modules:
  0.0 404.8 jit_solution(1170732939094853930)
XLA Ops:
  29.1 24.7 %all-to-all-start = ((f32[128,1,512]{2,1,0:T(1,128)}), f32[128,1,512]{2,1,0:T(1,128)S(1)}, u32[]{:S(2)}, u32[]{:S(2)}) async-start(f32[128,1,512]{2,1,0:T(1,128)} %reshape.483), calls=%async_computation | async-start | bytes 524288 | tf_op jit(solution)/shard_map/all_to_all | solution.py:15
  54.0 6.3 %all_gather.3 = f32[16,11,64]{2,1,0:T(8,128)S(1)} all-gather(f32[4,11,64]{2,1,0:T(8,128)S(1)} %pad_maximum_fusion.5), channel_id=1, replica_groups=mesh['leaf'=128,'sub'=4] {'sub'}, dimensions={0}, use_global_device_ids=true | all-gather | bytes 56320 | tf_op jit(solution)/shard_map/all_gather | solution.py:118
  60.5 10.1 %while.60 = (s32[]{:T(128)}, f32[4,8,64]{2,1,0:T(8,128)S(1)}, s32[4,6]{0,1:T(8,128)S(1)}, s32[]{:T(128)}, f32[16,8,64]{2,1,0:T(8,128)S(1)}, /*index=5*/f32[4,3,6...) while((s32[]{:T(128)}, f32[4,8,64]{2,1,0:T(8,128)S(1)}, s32[4,6]{0,1:T(8,128)S(1)}, ...), condition=%wide.region_5.6_spmd.clone, body=%wide.region_4.5_spmd.clone.sunk | while | flops 1727519 | bytes 69875 | solution.py:59
  75.1 113.0 %while.59 = (s32[]{:T(128)}, f32[32,8,64]{2,1,0:T(8,128)S(1)}, s32[32,20]{0,1:T(8,128)}, s32[]{:T(128)}, f32[96,8,64]{2,1,0:T(8,128)S(1)}, /*index=5*/f32[32,3,6...) while((s32[]{:T(128)}, f32[32,8,64]{2,1,0:T(8,128)S(1)}, s32[32,20]{0,1:T(8,128)}, ...), condition=%wide.region_3.4_spmd.clone, body=%wide.region_2.3_spmd.clone.sunk | while | flops 13812963 | bytes 529523 | solution.py:59
  189.8 194.2 %while.58 = (s32[]{:T(128)}, f32[32,8,128]{2,1,0:T(8,128)}, s32[32,27]{0,1:T(8,128)S(1)}, s32[]{:T(128)}, f32[96,11,128]{2,1,0:T(8,128)S(1)}, /*index=5*/f32[32,3,128]{2,0,1:T(8,128)S(1)}, s32[]{:T(128)}, s32[]{:T(128)}) while((s32[]{:T(128)}, f32[32,8,128]{2,1,0:T(8,128)}, s32[32,27]{0,1:T(8,128)S(1)}, s32[]{:T(128)}, ...), condition=%wide.region_1.2_spmd.clone, body=%wide.region_0.1_spmd.clone.sunk | while | flops 55149792 | bytes 1054059 | solution.py:93
  197.1 6.5 %fusion.156 = f32[32,8,128]{2,1,0:T(8,128)} fusion(f32[32,128]{1,0:T(8,128)S(1)} %bitcast.176, f32[32,128]{1,0:T(8,128)S(1)} %get-tuple-element.912, f32[32,128]{1,0:T(8,128)S(1)} %bitcast.175, f32[32,128]{1,0:T(8,128)S(1)} %get-tuple-element.914, f32[32,128]{1,0:T(8,128)S(1)} %bitcast.174, f32[32,128]{1,0:T(8,128)S(1)} %get-tuple-element.916, ...), kind=kOutput, calls=%fused_computation.17.clone.1 | convolution fusion | flops 55148544 | bytes 492033 | tf_op jit(solution)/shard_map/while/body/eval_jaxpr/lpq,lrq->lrp/dot_general | solution.py:90
  204.3 6.5 %fusion.156 = f32[32,8,128]{2,1,0:T(8,128)} fusion(f32[32,128]{1,0:T(8,128)S(1)} %bitcast.176, f32[32,128]{1,0:T(8,128)S(1)} %get-tuple-element.912, f32[32,128]{1,0:T(8,128)S(1)} %bitcast.175, f32[32,128]{1,0:T(8,128)S(1)} %get-tuple-element.914, f32[32,128]{1,0:T(8,128)S(1)} %bitcast.174, f32[32,128]{1,0:T(8,128)S(1)} %get-tuple-element.916, ...), kind=kOutput, calls=%fused_computation.17.clone.1 | convolution fusion | flops 55148544 | bytes 492033 | tf_op jit(solution)/shard_map/while/body/eval_jaxpr/lpq,lrq->lrp/dot_general | solution.py:90
  211.5 6.5 %fusion.156 = f32[32,8,128]{2,1,0:T(8,128)} fusion(f32[32,128]{1,0:T(8,128)S(1)} %bitcast.176, f32[32,128]{1,0:T(8,128)S(1)} %get-tuple-element.912, f32[32,128]{1,0:T(8,128)S(1)} %bitcast.175, f32[32,128]{1,0:T(8,128)S(1)} %get-tuple-element.914, f32[32,128]{1,0:T(8,128)S(1)} %bitcast.174, f32[32,128]{1,0:T(8,128)S(1)} %get-tuple-element.916, ...), kind=kOutput, calls=%fused_computation.17.clone.1 | convolution fusion | flops 55148544 | bytes 492033 | tf_op jit(solution)/shard_map/while/body/eval_jaxpr/lpq,lrq->lrp/dot_general | solution.py:90
  218.7 6.5 %fusion.156 = f32[32,8,128]{2,1,0:T(8,128)} fusion(f32[32,128]{1,0:T(8,128)S(1)} %bitcast.176, f32[32,128]{1,0:T(8,128)S(1)} %get-tuple-element.912, f32[32,128]{1,0:T(8,128)S(1)} %bitcast.175, f32[32,128]{1,0:T(8,128)S(1)} %get-tuple-element.914, f32[32,128]{1,0:T(8,128)S(1)} %bitcast.174, f32[32,128]{1,0:T(8,128)S(1)} %get-tuple-element.916, ...), kind=kOutput, calls=%fused_computation.17.clone.1 | convolution fusion | flops 55148544 | bytes 492033 | tf_op jit(solution)/shard_map/while/body/eval_jaxpr/lpq,lrq->lrp/dot_general | solution.py:90
  225.9 6.5 %fusion.156 = f32[32,8,128]{2,1,0:T(8,128)} fusion(f32[32,128]{1,0:T(8,128)S(1)} %bitcast.176, f32[32,128]{1,0:T(8,128)S(1)} %get-tuple-element.912, f32[32,128]{1,0:T(8,128)S(1)} %bitcast.175, f32[32,128]{1,0:T(8,128)S(1)} %get-tuple-element.914, f32[32,128]{1,0:T(8,128)S(1)} %bitcast.174, f32[32,128]{1,0:T(8,128)S(1)} %get-tuple-element.916, ...), kind=kOutput, calls=%fused_computation.17.clone.1 | convolution fusion | flops 55148544 | bytes 492033 | tf_op jit(solution)/shard_map/while/body/eval_jaxpr/lpq,lrq->lrp/dot_general | solution.py:90
  233.2 6.5 %fusion.156 = f32[32,8,128]{2,1,0:T(8,128)} fusion(f32[32,128]{1,0:T(8,128)S(1)} %bitcast.176, f32[32,128]{1,0:T(8,128)S(1)} %get-tuple-element.912, f32[32,128]{1,0:T(8,128)S(1)} %bitcast.175, f32[32,128]{1,0:T(8,128)S(1)} %get-tuple-element.914, f32[32,128]{1,0:T(8,128)S(1)} %bitcast.174, f32[32,128]{1,0:T(8,128)S(1)} %get-tuple-element.916, ...), kind=kOutput, calls=%fused_computation.17.clone.1 | convolution fusion | flops 55148544 | bytes 492033 | tf_op jit(solution)/shard_map/while/body/eval_jaxpr/lpq,lrq->lrp/dot_general | solution.py:90
  240.4 6.5 %fusion.156 = f32[32,8,128]{2,1,0:T(8,128)} fusion(f32[32,128]{1,0:T(8,128)S(1)} %bitcast.176, f32[32,128]{1,0:T(8,128)S(1)} %get-tuple-element.912, f32[32,128]{1,0:T(8,128)S(1)} %bitcast.175, f32[32,128]{1,0:T(8,128)S(1)} %get-tuple-element.914, f32[32,128]{1,0:T(8,128)S(1)} %bitcast.174, f32[32,128]{1,0:T(8,128)S(1)} %get-tuple-element.916, ...), kind=kOutput, calls=%fused_computation.17.clone.1 | convolution fusion | flops 55148544 | bytes 492033 | tf_op jit(solution)/shard_map/while/body/eval_jaxpr/lpq,lrq->lrp/dot_general | solution.py:90
  247.6 6.5 %fusion.156 = f32[32,8,128]{2,1,0:T(8,128)} fusion(f32[32,128]{1,0:T(8,128)S(1)} %bitcast.176, f32[32,128]{1,0:T(8,128)S(1)} %get-tuple-element.912, f32[32,128]{1,0:T(8,128)S(1)} %bitcast.175, f32[32,128]{1,0:T(8,128)S(1)} %get-tuple-element.914, f32[32,128]{1,0:T(8,128)S(1)} %bitcast.174, f32[32,128]{1,0:T(8,128)S(1)} %get-tuple-element.916, ...), kind=kOutput, calls=%fused_computation.17.clone.1 | convolution fusion | flops 55148544 | bytes 492033 | tf_op jit(solution)/shard_map/while/body/eval_jaxpr/lpq,lrq->lrp/dot_general | solution.py:90
  254.8 6.5 %fusion.156 = f32[32,8,128]{2,1,0:T(8,128)} fusion(f32[32,128]{1,0:T(8,128)S(1)} %bitcast.176, f32[32,128]{1,0:T(8,128)S(1)} %get-tuple-element.912, f32[32,128]{1,0:T(8,128)S(1)} %bitcast.175, f32[32,128]{1,0:T(8,128)S(1)} %get-tuple-element.914, f32[32,128]{1,0:T(8,128)S(1)} %bitcast.174, f32[32,128]{1,0:T(8,128)S(1)} %get-tuple-element.916, ...), kind=kOutput, calls=%fused_computation.17.clone.1 | convolution fusion | flops 55148544 | bytes 492033 | tf_op jit(solution)/shard_map/while/body/eval_jaxpr/lpq,lrq->lrp/dot_general | solution.py:90
  262.0 6.5 %fusion.156 = f32[32,8,128]{2,1,0:T(8,128)} fusion(f32[32,128]{1,0:T(8,128)S(1)} %bitcast.176, f32[32,128]{1,0:T(8,128)S(1)} %get-tuple-element.912, f32[32,128]{1,0:T(8,128)S(1)} %bitcast.175, f32[32,128]{1,0:T(8,128)S(1)} %get-tuple-element.914, f32[32,128]{1,0:T(8,128)S(1)} %bitcast.174, f32[32,128]{1,0:T(8,128)S(1)} %get-tuple-element.916, ...), kind=kOutput, calls=%fused_computation.17.clone.1 | convolution fusion | flops 55148544 | bytes 492033 | tf_op jit(solution)/shard_map/while/body/eval_jaxpr/lpq,lrq->lrp/dot_general | solution.py:90
  269.2 6.5 %fusion.156 = f32[32,8,128]{2,1,0:T(8,128)} fusion(f32[32,128]{1,0:T(8,128)S(1)} %bitcast.176, f32[32,128]{1,0:T(8,128)S(1)} %get-tuple-element.912, f32[32,128]{1,0:T(8,128)S(1)} %bitcast.175, f32[32,128]{1,0:T(8,128)S(1)} %get-tuple-element.914, f32[32,128]{1,0:T(8,128)S(1)} %bitcast.174, f32[32,128]{1,0:T(8,128)S(1)} %get-tuple-element.916, ...), kind=kOutput, calls=%fused_computation.17.clone.1 | convolution fusion | flops 55148544 | bytes 492033 | tf_op jit(solution)/shard_map/while/body/eval_jaxpr/lpq,lrq->lrp/dot_general | solution.py:90
  276.5 6.5 %fusion.156 = f32[32,8,128]{2,1,0:T(8,128)} fusion(f32[32,128]{1,0:T(8,128)S(1)} %bitcast.176, f32[32,128]{1,0:T(8,128)S(1)} %get-tuple-element.912, f32[32,128]{1,0:T(8,128)S(1)} %bitcast.175, f32[32,128]{1,0:T(8,128)S(1)} %get-tuple-element.914, f32[32,128]{1,0:T(8,128)S(1)} %bitcast.174, f32[32,128]{1,0:T(8,128)S(1)} %get-tuple-element.916, ...), kind=kOutput, calls=%fused_computation.17.clone.1 | convolution fusion | flops 55148544 | bytes 492033 | tf_op jit(solution)/shard_map/while/body/eval_jaxpr/lpq,lrq->lrp/dot_general | solution.py:90
  283.7 6.5 %fusion.156 = f32[32,8,128]{2,1,0:T(8,128)} fusion(f32[32,128]{1,0:T(8,128)S(1)} %bitcast.176, f32[32,128]{1,0:T(8,128)S(1)} %get-tuple-element.912, f32[32,128]{1,0:T(8,128)S(1)} %bitcast.175, f32[32,128]{1,0:T(8,128)S(1)} %get-tuple-element.914, f32[32,128]{1,0:T(8,128)S(1)} %bitcast.174, f32[32,128]{1,0:T(8,128)S(1)} %get-tuple-element.916, ...), kind=kOutput, calls=%fused_computation.17.clone.1 | convolution fusion | flops 55148544 | bytes 492033 | tf_op jit(solution)/shard_map/while/body/eval_jaxpr/lpq,lrq->lrp/dot_general | solution.py:90
  290.9 6.5 %fusion.156 = f32[32,8,128]{2,1,0:T(8,128)} fusion(f32[32,128]{1,0:T(8,128)S(1)} %bitcast.176, f32[32,128]{1,0:T(8,128)S(1)} %get-tuple-element.912, f32[32,128]{1,0:T(8,128)S(1)} %bitcast.175, f32[32,128]{1,0:T(8,128)S(1)} %get-tuple-element.914, f32[32,128]{1,0:T(8,128)S(1)} %bitcast.174, f32[32,128]{1,0:T(8,128)S(1)} %get-tuple-element.916, ...), kind=kOutput, calls=%fused_computation.17.clone.1 | convolution fusion | flops 55148544 | bytes 492033 | tf_op jit(solution)/shard_map/while/body/eval_jaxpr/lpq,lrq->lrp/dot_general | solution.py:90
  298.1 6.5 %fusion.156 = f32[32,8,128]{2,1,0:T(8,128)} fusion(f32[32,128]{1,0:T(8,128)S(1)} %bitcast.176, f32[32,128]{1,0:T(8,128)S(1)} %get-tuple-element.912, f32[32,128]{1,0:T(8,128)S(1)} %bitcast.175, f32[32,128]{1,0:T(8,128)S(1)} %get-tuple-element.914, f32[32,128]{1,0:T(8,128)S(1)} %bitcast.174, f32[32,128]{1,0:T(8,128)S(1)} %get-tuple-element.916, ...), kind=kOutput, calls=%fused_computation.17.clone.1 | convolution fusion | flops 55148544 | bytes 492033 | tf_op jit(solution)/shard_map/while/body/eval_jaxpr/lpq,lrq->lrp/dot_general | solution.py:90
  305.3 6.5 %fusion.156 = f32[32,8,128]{2,1,0:T(8,128)} fusion(f32[32,128]{1,0:T(8,128)S(1)} %bitcast.176, f32[32,128]{1,0:T(8,128)S(1)} %get-tuple-element.912, f32[32,128]{1,0:T(8,128)S(1)} %bitcast.175, f32[32,128]{1,0:T(8,128)S(1)} %get-tuple-element.914, f32[32,128]{1,0:T(8,128)S(1)} %bitcast.174, f32[32,128]{1,0:T(8,128)S(1)} %get-tuple-element.916, ...), kind=kOutput, calls=%fused_computation.17.clone.1 | convolution fusion | flops 55148544 | bytes 492033 | tf_op jit(solution)/shard_map/while/body/eval_jaxpr/lpq,lrq->lrp/dot_general | solution.py:90
  312.6 6.5 %fusion.156 = f32[32,8,128]{2,1,0:T(8,128)} fusion(f32[32,128]{1,0:T(8,128)S(1)} %bitcast.176, f32[32,128]{1,0:T(8,128)S(1)} %get-tuple-element.912, f32[32,128]{1,0:T(8,128)S(1)} %bitcast.175, f32[32,128]{1,0:T(8,128)S(1)} %get-tuple-element.914, f32[32,128]{1,0:T(8,128)S(1)} %bitcast.174, f32[32,128]{1,0:T(8,128)S(1)} %get-tuple-element.916, ...), kind=kOutput, calls=%fused_computation.17.clone.1 | convolution fusion | flops 55148544 | bytes 492033 | tf_op jit(solution)/shard_map/while/body/eval_jaxpr/lpq,lrq->lrp/dot_general | solution.py:90
  319.8 6.5 %fusion.156 = f32[32,8,128]{2,1,0:T(8,128)} fusion(f32[32,128]{1,0:T(8,128)S(1)} %bitcast.176, f32[32,128]{1,0:T(8,128)S(1)} %get-tuple-element.912, f32[32,128]{1,0:T(8,128)S(1)} %bitcast.175, f32[32,128]{1,0:T(8,128)S(1)} %get-tuple-element.914, f32[32,128]{1,0:T(8,128)S(1)} %bitcast.174, f32[32,128]{1,0:T(8,128)S(1)} %get-tuple-element.916, ...), kind=kOutput, calls=%fused_computation.17.clone.1 | convolution fusion | flops 55148544 | bytes 492033 | tf_op jit(solution)/shard_map/while/body/eval_jaxpr/lpq,lrq->lrp/dot_general | solution.py:90
  327.0 6.5 %fusion.156 = f32[32,8,128]{2,1,0:T(8,128)} fusion(f32[32,128]{1,0:T(8,128)S(1)} %bitcast.176, f32[32,128]{1,0:T(8,128)S(1)} %get-tuple-element.912, f32[32,128]{1,0:T(8,128)S(1)} %bitcast.175, f32[32,128]{1,0:T(8,128)S(1)} %get-tuple-element.914, f32[32,128]{1,0:T(8,128)S(1)} %bitcast.174, f32[32,128]{1,0:T(8,128)S(1)} %get-tuple-element.916, ...), kind=kOutput, calls=%fused_computation.17.clone.1 | convolution fusion | flops 55148544 | bytes 492033 | tf_op jit(solution)/shard_map/while/body/eval_jaxpr/lpq,lrq->lrp/dot_general | solution.py:90
  334.2 6.5 %fusion.156 = f32[32,8,128]{2,1,0:T(8,128)} fusion(f32[32,128]{1,0:T(8,128)S(1)} %bitcast.176, f32[32,128]{1,0:T(8,128)S(1)} %get-tuple-element.912, f32[32,128]{1,0:T(8,128)S(1)} %bitcast.175, f32[32,128]{1,0:T(8,128)S(1)} %get-tuple-element.914, f32[32,128]{1,0:T(8,128)S(1)} %bitcast.174, f32[32,128]{1,0:T(8,128)S(1)} %get-tuple-element.916, ...), kind=kOutput, calls=%fused_computation.17.clone.1 | convolution fusion | flops 55148544 | bytes 492033 | tf_op jit(solution)/shard_map/while/body/eval_jaxpr/lpq,lrq->lrp/dot_general | solution.py:90
  341.4 6.5 %fusion.156 = f32[32,8,128]{2,1,0:T(8,128)} fusion(f32[32,128]{1,0:T(8,128)S(1)} %bitcast.176, f32[32,128]{1,0:T(8,128)S(1)} %get-tuple-element.912, f32[32,128]{1,0:T(8,128)S(1)} %bitcast.175, f32[32,128]{1,0:T(8,128)S(1)} %get-tuple-element.914, f32[32,128]{1,0:T(8,128)S(1)} %bitcast.174, f32[32,128]{1,0:T(8,128)S(1)} %get-tuple-element.916, ...), kind=kOutput, calls=%fused_computation.17.clone.1 | convolution fusion | flops 55148544 | bytes 492033 | tf_op jit(solution)/shard_map/while/body/eval_jaxpr/lpq,lrq->lrp/dot_general | solution.py:90
  348.6 6.5 %fusion.156 = f32[32,8,128]{2,1,0:T(8,128)} fusion(f32[32,128]{1,0:T(8,128)S(1)} %bitcast.176, f32[32,128]{1,0:T(8,128)S(1)} %get-tuple-element.912, f32[32,128]{1,0:T(8,128)S(1)} %bitcast.175, f32[32,128]{1,0:T(8,128)S(1)} %get-tuple-element.914, f32[32,128]{1,0:T(8,128)S(1)} %bitcast.174, f32[32,128]{1,0:T(8,128)S(1)} %get-tuple-element.916, ...), kind=kOutput, calls=%fused_computation.17.clone.1 | convolution fusion | flops 55148544 | bytes 492033 | tf_op jit(solution)/shard_map/while/body/eval_jaxpr/lpq,lrq->lrp/dot_general | solution.py:90
  355.9 6.5 %fusion.156 = f32[32,8,128]{2,1,0:T(8,128)} fusion(f32[32,128]{1,0:T(8,128)S(1)} %bitcast.176, f32[32,128]{1,0:T(8,128)S(1)} %get-tuple-element.912, f32[32,128]{1,0:T(8,128)S(1)} %bitcast.175, f32[32,128]{1,0:T(8,128)S(1)} %get-tuple-element.914, f32[32,128]{1,0:T(8,128)S(1)} %bitcast.174, f32[32,128]{1,0:T(8,128)S(1)} %get-tuple-element.916, ...), kind=kOutput, calls=%fused_computation.17.clone.1 | convolution fusion | flops 55148544 | bytes 492033 | tf_op jit(solution)/shard_map/while/body/eval_jaxpr/lpq,lrq->lrp/dot_general | solution.py:90
  363.1 6.5 %fusion.156 = f32[32,8,128]{2,1,0:T(8,128)} fusion(f32[32,128]{1,0:T(8,128)S(1)} %bitcast.176, f32[32,128]{1,0:T(8,128)S(1)} %get-tuple-element.912, f32[32,128]{1,0:T(8,128)S(1)} %bitcast.175, f32[32,128]{1,0:T(8,128)S(1)} %get-tuple-element.914, f32[32,128]{1,0:T(8,128)S(1)} %bitcast.174, f32[32,128]{1,0:T(8,128)S(1)} %get-tuple-element.916, ...), kind=kOutput, calls=%fused_computation.17.clone.1 | convolution fusion | flops 55148544 | bytes 492033 | tf_op jit(solution)/shard_map/while/body/eval_jaxpr/lpq,lrq->lrp/dot_general | solution.py:90
  370.3 6.5 %fusion.156 = f32[32,8,128]{2,1,0:T(8,128)} fusion(f32[32,128]{1,0:T(8,128)S(1)} %bitcast.176, f32[32,128]{1,0:T(8,128)S(1)} %get-tuple-element.912, f32[32,128]{1,0:T(8,128)S(1)} %bitcast.175, f32[32,128]{1,0:T(8,128)S(1)} %get-tuple-element.914, f32[32,128]{1,0:T(8,128)S(1)} %bitcast.174, f32[32,128]{1,0:T(8,128)S(1)} %get-tuple-element.916, ...), kind=kOutput, calls=%fused_computation.17.clone.1 | convolution fusion | flops 55148544 | bytes 492033 | tf_op jit(solution)/shard_map/while/body/eval_jaxpr/lpq,lrq->lrp/dot_general | solution.py:90
  377.5 6.5 %fusion.156 = f32[32,8,128]{2,1,0:T(8,128)} fusion(f32[32,128]{1,0:T(8,128)S(1)} %bitcast.176, f32[32,128]{1,0:T(8,128)S(1)} %get-tuple-element.912, f32[32,128]{1,0:T(8,128)S(1)} %bitcast.175, f32[32,128]{1,0:T(8,128)S(1)} %get-tuple-element.914, f32[32,128]{1,0:T(8,128)S(1)} %bitcast.174, f32[32,128]{1,0:T(8,128)S(1)} %get-tuple-element.916, ...), kind=kOutput, calls=%fused_computation.17.clone.1 | convolution fusion | flops 55148544 | bytes 492033 | tf_op jit(solution)/shard_map/while/body/eval_jaxpr/lpq,lrq->lrp/dot_general | solution.py:90
  386.0 13.1 %while.61 = (s32[]{:T(128)}, f32[1,8,64]{2,1,0:T(8,128)S(1)}, s32[1,6]{1,0:T(1,128)S(1)}, f32[128,8,64]{2,1,0:T(8,128)S(1)}, f32[1,3,64]{2,1,0:T(4,128)S(1)}, /*...) while((s32[]{:T(128)}, f32[1,8,64]{2,1,0:T(8,128)S(1)}, ...), condition=%wide.region_8.9_spmd.clone, body=%wide.region_7.8_spmd.clone.sunk | while | flops 431623 | bytes 18109 | solution.py:59
  (481 shorter events, 193.8 us)
Async XLA Ops:
  0.0 22.0 %copy-start = (f32[32,64,64]{2,1,0:T(8,128)S(1)}, f32[32,64,64]{2,1,0:T(8,128)}, u32[]{:S(2)}) copy-start(f32[32,64,64]{2,1,0:T(8,128)} %param.24) | copy-start | bytes 1572868
  2.4 3.5 copy-start.12
  2.4 14.4 %copy-start.2 = (f32[32,3,128]{2,0,1:T(8,128)S(1)}, f32[32,3,128]{2,0,1:T(8,128)}, u32[]{:S(2)}) copy-start(f32[32,3,128]{2,0,1:T(8,128)} %param.19) | copy-start | bytes 147460
  2.4 14.5 %copy-start.3 = (f32[32,8,128]{2,1,0:T(8,128)S(1)}, f32[32,8,128]{2,1,0:T(8,128)}, u32[]{:S(2)}) copy-start(f32[32,8,128]{2,1,0:T(8,128)} %param.20) | copy-start | bytes 393220
  5.9 16.7 %copy-start.4 = (f32[4,64,64]{2,1,0:T(8,128)S(1)}, f32[4,64,64]{2,1,0:T(8,128)}, u32[]{:S(2)}) copy-start(f32[4,64,64]{2,1,0:T(8,128)} %param.25) | copy-start | bytes 196612
  6.0 65.5 %collective-permute-start.2 = (f32[32,11,64]{2,1,0:T(8,128)S(1)}, f32[32,11,64]{2,1,0:T(8,128)}, u32[]{:S(2)}, u32[]{:S(2)}) collective-permute-start(f32[32,11,64]{2,1,0:T(8,128)S(1)} %pad_maximum_fusion.3), channel_id=1, source_target_pairs={{0,1},{1,2},{2,3},{3,4},{4,5},{5,6},{6,7},{7,8},{8,9},{9,10},{10,1... | collective-permute-start | bytes 270344 | tf_op jit(solution)/shard_map/ppermute | solution.py:27
  10.6 62.0 %collective-permute-start.3 = (f32[32,11,64]{2,1,0:T(8,128)S(1)}, f32[32,11,64]{2,1,0:T(8,128)}, u32[]{:S(2)}, u32[]{:S(2)}) collective-permute-start(f32[32,11,64]{2,1,0:T(8,128)S(1)} %pad_maximum_fusion.3), channel_id=1, source_target_pairs={{1,0},{2,1},{3,2},{4,3},{5,4},{6,5},{7,6},{8,7},{9,8},{10,9},{11,1... | collective-permute-start | bytes 270344 | tf_op jit(solution)/shard_map/ppermute | solution.py:30
  17.0 171.1 %collective-permute-start = (f32[32,11,128]{2,1,0:T(8,128)S(1)}, f32[32,11,128]{2,1,0:T(8,128)}, u32[]{:S(2)}, u32[]{:S(2)}) collective-permute-start(f32[32,11,128]{2,1,0:T(8,128)S(1)} %pad_maximum_fusion.2), channel_id=1, source_target_pairs={{0,1},{1,2},{2,3},{3,4},{4,5},{5,6},{6,7},{7,8},{8,9},{9,10},{10,1... | collective-permute-start | bytes 540680 | tf_op jit(solution)/shard_map/ppermute | solution.py:27
  18.9 169.8 %collective-permute-start.1 = (f32[32,11,128]{2,1,0:T(8,128)S(1)}, f32[32,11,128]{2,1,0:T(8,128)}, u32[]{:S(2)}, u32[]{:S(2)}) collective-permute-start(f32[32,11,128]{2,1,0:T(8,128)S(1)} %pad_maximum_fusion.2), channel_id=1, source_target_pairs={{1,0},{2,1},{3,2},{4,3},{5,4},{6,5},{7,6},{8,7},{9,8},{10,9},{11,1... | collective-permute-start | bytes 540680 | tf_op jit(solution)/shard_map/ppermute | solution.py:30
  28.1 26.0 %copy-start.5 = (f32[4,3,64]{2,0,1:T(4,128)S(1)}, f32[4,3,64]{2,0,1:T(4,128)}, u32[]{:S(2)}) copy-start(f32[4,3,64]{2,0,1:T(4,128)} %param.22) | copy-start | bytes 9220
  28.1 32.4 %copy-start.17 = (s32[4,6]{1,0:T(4,128)S(1)}, s32[4,6]{1,0:T(4,128)}, u32[]{:S(2)}) copy-start(s32[4,6]{1,0:T(4,128)} %param.28) | copy-start | bytes 292
  29.1 354.9 %all-to-all-start = ((f32[128,1,512]{2,1,0:T(1,128)}), f32[128,1,512]{2,1,0:T(1,128)S(1)}, u32[]{:S(2)}, u32[]{:S(2)}) async-start(f32[128,1,512]{2,1,0:T(1,128)} %reshape.483), calls=%async_computation | async-start | bytes 524288 | tf_op jit(solution)/shard_map/all_to_all | solution.py:15
  60.5 10.7 %copy-start.10 = (f32[128,3,64]{0,2,1:T(8,128)S(1)}, f32[128,3,64]{0,2,1:T(8,128)}, u32[]{:S(2)}) copy-start(f32[128,3,64]{0,2,1:T(8,128)} %param.23) | copy-start | bytes 294916
  60.5 10.8 %copy-start.11 = (s32[32,27]{1,0:T(8,128)S(1)}, s32[32,27]{1,0:T(8,128)}, u32[]{:S(2)}) copy-start(s32[32,27]{1,0:T(8,128)} %param.26) | copy-start | bytes 10372
  70.6 0.6 copy-start.14
  74.0 0.8 copy-start.1
  74.1 0.9 copy-start.7
  188.1 0.7 copy-start.8
  384.0 2.0 copy-start.16
  385.9 13.3 %copy-start.15 = (f32[4,8,64]{2,1,0:T(8,128)S(1)}, f32[4,8,64]{2,1,0:T(8,128)}, u32[]{:S(2)}) copy-start(f32[4,8,64]{2,1,0:T(8,128)} %copy-done.14) | copy-start | bytes 24580
  386.0 16.1 %copy-start.9 = (f32[32,8,64]{2,1,0:T(8,128)S(1)}, f32[32,8,64]{2,1,0:T(8,128)}, u32[]{:S(2)}) copy-start(f32[32,8,64]{2,1,0:T(8,128)} %copy-done.8) | copy-start | bytes 196612
  399.2 3.0 copy-start.13
  402.2 1.9 copy-start.6
